TPU v7x, 32 devices: a whole 2x2x4 slice. The times are simulated.
32 devices in a mesh: parts: 2 (over y), shard: 4 (over z), grp: 2 (over x), rep: 2 (over core).
Axes of the slice: x: 2, y: 2, z: 4, core: 2. Of those that a mesh axis runs over, the one named last changes fastest.
Arguments:
- embeddings: float32 [4096, 768], P(('parts', 'shard', 'grp', 'rep')), parts along dimension 0, may hold values from -6 to 6
- clusters: int32 [4096, 1], P(('parts', 'shard', 'grp', 'rep')), parts along dimension 0, may hold values from 0 to 7; in each aligned block of 128 rows (0 to 127, 128 to 255, ...) at most 32 rows name the same one
Outputs:
- dup_weight: float32 [4096], P(('parts', 'shard', 'grp', 'rep')), parts along dimension 0
There are 2 independent parts, one for each index of `parts`. A program takes and returns all parts, laid end to end along the dimension named above; each array names one. Nothing has to cross between parts.
Inputs may be any that keep to these rules, and one draw needn't show every extreme that they name: `clusters`: among the rows of one device, at most 32 belong to any one cluster, and some cluster has exactly 32 of them.
All inputs are finite; a program needn't handle non-finite values.
Results may differ from a plain program's by a relative error of at most 0.00035.
Values may be sent and summed in bfloat16 or wider, within the bound.
A program may use at most 64 MiB of HBM per device.

v0:
```python
import jax
import jax.numpy as jnp
from jax import lax
from jax.sharding import PartitionSpec as P

sharpness = 60.0


def from_partner(value, axis, distance):
    mask = 2**distance
    pairs = [(source, source ^ mask) for source in range(lax.axis_size(axis))]
    return lax.ppermute(value, axis, pairs)


def unit_rows(matrix):
    inverse = lax.rsqrt(jnp.sum(matrix * matrix, axis=1, keepdims=True) + 1e-06)
    return (matrix * inverse).astype(jnp.bfloat16)


def body(embeddings, clusters):
    shard_count = lax.axis_size("shard")
    group_count = lax.axis_size("grp")
    owners = shard_count * group_count
    row_count = embeddings.shape[0]
    feature_dim = embeddings.shape[1]
    capacity = 2 * row_count // owners
    normed = unit_rows(embeddings)
    cluster_of = clusters[:, 0]
    member_table = (cluster_of[:, None] == jnp.arange(owners, dtype=jnp.int32)[None, :]).astype(
        jnp.float32
    )
    earlier = (jnp.arange(row_count)[:, None] > jnp.arange(row_count)[None, :]).astype(jnp.float32)
    preceding = jnp.dot(
        earlier, member_table, precision=lax.Precision.HIGHEST, preferred_element_type=jnp.float32
    )
    position = jnp.sum(preceding * member_table, axis=1).astype(jnp.int32)
    slot_index = cluster_of * capacity + position
    outgoing = jnp.zeros((owners * capacity, feature_dim), jnp.bfloat16).at[slot_index].set(normed)
    present = jnp.zeros((owners * capacity,), jnp.int32).at[slot_index].set(1)
    arrived, arrived_live = (
        lax.all_to_all(
            outgoing.reshape(owners, capacity, feature_dim),
            ("shard", "grp"),
            split_axis=0,
            concat_axis=0,
            tiled=True,
        ),
        lax.all_to_all(
            present.reshape(owners, capacity),
            ("shard", "grp"),
            split_axis=0,
            concat_axis=0,
            tiled=True,
        ),
    )
    slot_count = owners * capacity
    local_rows = arrived.reshape(slot_count, feature_dim)
    local_live = arrived_live.reshape(slot_count)
    partner, partner_live = from_partner((local_rows, local_live), "rep", 0)
    key_rows = jnp.concatenate([local_rows, partner], axis=0)
    key_live = jnp.concatenate([local_live, partner_live], axis=0) > 0
    key_pos = jnp.arange(2 * slot_count, dtype=jnp.int32)

    def block_sums(block_index):
        first_row = block_index * slot_count
        scores = lax.dot_general(
            local_rows, key_rows, (((1,), (1,)), ((), ())), preferred_element_type=jnp.float32
        )
        query_pos = first_row + jnp.arange(slot_count, dtype=jnp.int32)
        paired = key_live[None, :] & (query_pos[:, None] != key_pos[None, :])
        return jnp.sum(jnp.where(paired, jnp.exp(sharpness * scores), 0.0), axis=1)

    partial_mass = lax.map(
        block_sums, jnp.arange(slot_count // slot_count, dtype=jnp.int32)
    ).reshape(slot_count)
    returned = lax.all_to_all(
        partial_mass.reshape(owners, capacity),
        ("shard", "grp"),
        split_axis=0,
        concat_axis=0,
        tiled=True,
    )
    mass = returned.reshape(slot_count)[slot_index]
    return jnp.log1p(mass)


def solution(mesh):
    placed = (P(("parts", "shard", "grp", "rep"), None), P(("parts", "shard", "grp", "rep"), None))
    return jax.shard_map(
        body,
        mesh=mesh,
        in_specs=placed,
        out_specs=P(("parts", "shard", "grp", "rep")),
        check_vma=False,
    )
```

profile of v0, /device:TPU:0, one launch (start us, length us, event | category | flops | bytes accessed | tf_op | source)
XLA Modules:
  0.0 50.2 jit_solution(17838194070103447882)
XLA Ops:
  0.0 0.0 copy-start
  0.0 0.9 %fusion.1 = f32[128]{0:T(128)S(1)} fusion(s32[128]{0:T(128)} %bitcast.13), kind=kOutput, calls=%fused_computation.6 | convolution fusion | flops 282496 | bytes 1024 | tf_op jit(solution)/shard_map/dot_general | solution.py:33
  0.9 0.7 %fusion.12 = s32[128]{0:T(128)S(1)} fusion(f32[128]{0:T(128)S(1)} %fusion.1, s32[128,1]{0,1:T(1,128)} %param.3), kind=kLoop, calls=%fused_computation.24 | loop fusion | flops 768 | bytes 1536 | tf_op jit(solution)/shard_map/select_n | solution.py:38
  1.6 1.1 %multiply_reduce_fusion = f32[128]{0:T(128)S(1)} fusion(f32[128,768]{1,0:T(8,128)} %param.2), kind=kLoop, calls=%fused_computation.14 | loop fusion | flops 196480 | bytes 393728 | tf_op jit(solution)/shard_map/reduce_sum | solution.py:16
  2.7 0.0 copy-done
  2.7 1.3 %scatter_custom_fusion.1 = bf16[256,768]{1,0:T(8,128)(2,1)S(1)} fusion(s32[128]{0:T(128)S(1)} %fusion.12, f32[128,768]{1,0:T(8,128)S(1)} %copy-done, f32[128]{0:T(128)S(1)} %add_rsqrt_fusion, bf16[]{:T(256)} %constant.15.clone.1), kind=kCustom, calls=%fused_computation.15 | custom fusion | flops 196608 | bytes 786946 | tf_op jit(solution)/shard_map/scatter | solution.py:38
  4.0 19.1 %all_to_all.23 = bf16[8,32,768]{2,1,0:T(8,128)(2,1)S(1)} all-to-all(bf16[8,32,768]{2,1,0:T(8,128)(2,1)S(1)} %bitcast.10), channel_id=1, replica_groups=mesh['parts'=2,'shard'=4,'grp'=2,'rep'=2] {'shard','grp'}, dimensions={0} | all-to-all | bytes 786432 | tf_op jit(solution)/shard_map/all_to_all | solution.py:41
  23.1 0.0 collective-permute-start.1
  23.1 1.0 %scatter_custom_fusion = s32[256]{0:T(256)S(1)} fusion(s32[128]{0:T(128)S(1)} %fusion.12, s32[128]{0:T(128)S(1)} %broadcast.30, s32[]{:T(128)} %constant.10.clone.1), kind=kCustom, calls=%fused_computation.27 | custom fusion | bytes 1028 | tf_op jit(solution)/shard_map/scatter | solution.py:39
  24.1 0.1 all_to_all.15
  24.2 9.5 %all_to_all.24 = s32[8,1,32]{2,1,0:T(1,128)S(1)} all-to-all(s32[8,1,32]{2,1,0:T(1,128)S(1)} %all_to_all.15), channel_id=1, replica_groups=mesh['parts'=2,'shard'=4,'grp'=2,'rep'=2] {'shard','grp'}, dimensions={0} | all-to-all | bytes 2048 | tf_op jit(solution)/shard_map/all_to_all | solution.py:48
  33.7 0.5 %broadcast.47 = s32[]{:T(128)} broadcast(s32[]{:T(128)} %constant.10.clone.1), dimensions={} | broadcast | bytes 8 | tf_op jit(solution)/shard_map/all_to_all | solution.py:48
  34.3 0.7 %reduce.6 = s32[8,32]{1,0:T(8,128)S(1)} reduce(s32[8,1,32]{2,1,0:T(1,128)S(1)} %all_to_all.24, s32[]{:T(128)} %broadcast.47), dimensions={1}, to_apply=%all_to_all.16.reduce_sub_computation.3 | reduce | bytes 2052 | tf_op jit(solution)/shard_map/all_to_all | solution.py:48
  34.9 0.1 concatenate.12
  35.0 0.0 collective-permute-start
  35.0 1.1 %collective-permute-done = s32[256]{0:T(256)S(1)} collective-permute-done((s32[256]{0:T(256)S(1)}, s32[256]{0:T(256)S(1)}, u32[]{:S(2)}, u32[]{:S(2)}) %collective-permute-start) | collective-permute-done | bytes 1056 | tf_op jit(solution)/shard_map/ppermute | solution.py:12
  36.2 0.0 collective-permute-done.1
  36.2 0.5 %select_reduce_fusion = f32[256]{0:T(256)S(1)} fusion(bf16[256,768]{1,0:T(8,128)(2,1)S(1)} %bitcast.12, bf16[256,768]{1,0:T(8,128)(2,1)S(1)} %collective-permute-done.1, pred[512]{0:T(512)(128)(4,1)S(1)} %add_compare_fusion), kind=kOutput, calls=%fused_computation.10 | convolution fusion | flops 203554560 | bytes 787968 | tf_op jit(solution)/shard_map/while/body/eval_jaxpr/dot_general | solution.py:66
  36.7 0.7 %all_to_all.18 = f32[8,1,32]{2,1,0:T(1,128)} reshape(f32[256]{0:T(256)S(1)} %select_reduce_fusion) | data formatting | bytes 2048 | tf_op jit(solution)/shard_map/all_to_all | solution.py:76
  37.4 3.3 %all-to-all-start.2 = ((f32[8,1,32]{2,1,0:T(1,128)}), f32[8,1,32]{2,1,0:T(1,128)S(1)}, u32[]{:S(2)}, u32[]{:S(2)}) async-start(f32[8,1,32]{2,1,0:T(1,128)} %all_to_all.18), calls=%async_computation.2 | async-start | bytes 8192 | tf_op jit(solution)/shard_map/all_to_all | solution.py:76
  40.7 6.4 %all-to-all-done.2 = f32[8,1,32]{2,1,0:T(1,128)S(1)} async-done(((f32[8,1,32]{2,1,0:T(1,128)}), f32[8,1,32]{2,1,0:T(1,128)S(1)}, u32[]{:S(2)}, u32[]{:S(2)}) %all-to-all-start.2) | async-done | bytes 1056 | tf_op jit(solution)/shard_map/all_to_all | solution.py:76
  47.2 0.5 %broadcast.48 = f32[]{:T(128)} broadcast(f32[]{:T(128)} %constant.68), dimensions={} | broadcast | bytes 8 | tf_op jit(solution)/shard_map/all_to_all | solution.py:76
  47.7 0.7 %reduce.7 = f32[8,32]{1,0:T(8,128)S(1)} reduce(f32[8,1,32]{2,1,0:T(1,128)S(1)} %all-to-all-done.2, f32[]{:T(128)} %broadcast.48), dimensions={1}, to_apply=%all_to_all.19.reduce_sub_computation.3 | reduce | bytes 2052 | tf_op jit(solution)/shard_map/all_to_all | solution.py:76
  48.3 0.1 reshape.53
  48.4 1.3 %gather_fusion = f32[128]{0:T(128)S(1)} fusion(f32[256]{0:T(256)S(1)} %reshape.53, s32[1024]{0:T(1024)S(1)} %pad_clamp_fusion), kind=kCustom, calls=%fused_computation | custom fusion | bytes 1536 | tf_op jit(solution)/shard_map/gather | solution.py:83
  49.7 0.5 %log1p.3 = f32[128]{0:T(128)} log-plus-one(f32[128]{0:T(128)S(1)} %gather_fusion) | non-fusion elementwise | bytes 1024 | tf_op jit(solution)/shard_map/log1p | solution.py:84
  (4 shorter events, 0.0 us)
Async XLA Ops:
  0.0 2.7 %copy-start = (f32[128,768]{1,0:T(8,128)S(1)}, f32[128,768]{1,0:T(8,128)}, u32[]{:S(2)}) copy-start(f32[128,768]{1,0:T(8,128)} %param.2) | copy-start | bytes 1179652
  23.1 13.1 %collective-permute-start.1 = (bf16[256,768]{1,0:T(8,128)(2,1)S(1)}, bf16[256,768]{1,0:T(8,128)(2,1)S(1)}, u32[]{:S(2)}, u32[]{:S(2)}) collective-permute-start(bf16[256,768]{1,0:T(8,128)(2,1)S(1)} %bitcast.11), channel_id=1, source_target_pairs={{0,1},{1,0},{2,3},{3,2},{4,5},{5,4},{6,7},{7,6},{8,9},{9,8},{10,11... | collective-permute-start | bytes 1179656 | tf_op jit(solution)/shard_map/ppermute | solution.py:12
  35.0 1.2 %collective-permute-start = (s32[256]{0:T(256)S(1)}, s32[256]{0:T(256)S(1)}, u32[]{:S(2)}, u32[]{:S(2)}) collective-permute-start(s32[256]{0:T(256)S(1)} %concatenate.12), channel_id=1, source_target_pairs={{0,1},{1,0},{2,3},{3,2},{4,5},{5,4},{6,7},{7,6},{8,9},{9,8},{10,11... | collective-permute-start | bytes 3080 | tf_op jit(solution)/shard_map/ppermute | solution.py:12
  37.4 9.8 %all-to-all-start.2 = ((f32[8,1,32]{2,1,0:T(1,128)}), f32[8,1,32]{2,1,0:T(1,128)S(1)}, u32[]{:S(2)}, u32[]{:S(2)}) async-start(f32[8,1,32]{2,1,0:T(1,128)} %all_to_all.18), calls=%async_computation.2 | async-start | bytes 8192 | tf_op jit(solution)/shard_map/all_to_all | solution.py:76
where the time goes:
time: 50.5 us; the launch traced here: 50.2 us
  blocking collectives  28.7 us (57%)
  waiting for transfers between devices  7.57 us (15%)
  local copies, waits for them, and re-layouts  4.71 us (9%)
  other arithmetic  4.43 us (9%)
  starting transfers between devices  3.34 us (7%)
  matrix products  1.39 us (3%)
    all_to_all x1, blocking collectives, body(): lax.all_to_all(outgoing.reshape(owners, capacity, feature_dim), ('shard',...  19.1 us
    all_to_all x1, blocking collectives, body(): lax.all_to_all(present.reshape(owners, capacity), ('shard', 'grp'), split...  9.54 us
    all_to_all x1, waiting for transfers between devices, body(): lax.all_to_all(partial_mass.reshape(owners, capacity), ('shard', 'grp'),...  6.42 us
    all_to_all x1, starting transfers between devices, body(): lax.all_to_all(partial_mass.reshape(owners, capacity), ('shard', 'grp'),...  3.33 us
    scatter x1, other arithmetic, body(): jnp.zeros((owners * capacity, feature_dim), jnp.bfloat16).at[slot_index]  1.31 us
    gather x1, local copies, waits for them, and re-layouts, body(): mass = returned.reshape(slot_count)[slot_index]  1.26 us
    all_to_all x2, local copies, waits for them, and re-layouts, body(): lax.all_to_all(partial_mass.reshape(owners, capacity), ('shard', 'grp'),...  1.2 us
    ppermute x2, waiting for transfers between devices, from_partner(): return lax.ppermute(value, axis, pairs)  1.15 us
  transfers between devices with their start and end apart: 3, of which 2 were waited for; matrix products, arithmetic and copies ran while one was open for 4% of the time, Pallas kernels for 0%

commit v1 on v0

--- a/solution.py
+++ b/solution.py
@@ -1,6 +1,10 @@
+import functools
+
 import jax
 import jax.numpy as jnp
 from jax import lax
+from jax.experimental import pallas as pl
+from jax.experimental.pallas import tpu as pltpu
 from jax.sharding import PartitionSpec as P
 
 sharpness = 60.0
@@ -17,7 +21,7 @@
     return (matrix * inverse).astype(jnp.bfloat16)
 
 
-def body(embeddings, clusters):
+def collective_body(embeddings, clusters):
     shard_count = lax.axis_size("shard")
     group_count = lax.axis_size("grp")
     owners = shard_count * group_count
@@ -84,8 +88,222 @@
     return jnp.log1p(mass)
 
 
+def ring_distance(step, size):
+    return min(step, size - step)
+
+
+def kernel(sizes, capacity, rows_hbm, cluster_ref, mass_ref, rows, outgoing, gathered, mass, returned,
+           load_sem, send_sem, recv_sem, reply_send_sem, reply_recv_sem):
+    n_shard, n_grp, n_rep = sizes
+    shard, grp, rep = lax.axis_index("shard"), lax.axis_index("grp"), lax.axis_index("rep")
+    row_count, width = rows.shape
+    per_row = mass.shape[2] // capacity
+    steps = [(a, b) for a in range(n_shard) for b in range(n_grp)]
+    steps.sort(key=lambda s: -(ring_distance(s[0], n_shard) + ring_distance(s[1], n_grp)))
+    away = steps[:-1]
+    home = len(away)
+
+    def chip(step):
+        return lax.rem(shard + step[0], n_shard), lax.rem(grp + step[1], n_grp)
+
+    def owner_of(step):
+        z, x = chip(step)
+        return z * n_grp + x
+
+    def device(step, core):
+        z, x = chip(step)
+        return {"shard": z, "grp": x, "rep": core}
+
+    my_owner = shard * n_grp + grp
+    me = my_owner * n_rep + rep
+
+    load = pltpu.make_async_copy(rows_hbm, rows, load_sem)
+    load.start()
+    barrier = pltpu.get_barrier_semaphore()
+
+    def greet(step, core):
+        pl.semaphore_signal(barrier, inc=1, device_id=device(step, core))
+
+    for step in away:
+        greet(step, 0)
+
+    @pl.when(rep == 0)
+    def _():
+        for core in range(1, n_rep):
+            for step in steps:
+                greet(step, core)
+
+    @pl.when(rep != 0)
+    def _():
+        greet((0, 0), 0)
+
+    square = (row_count, row_count)
+    down = lax.broadcasted_iota(jnp.int32, square, 0)
+    across = lax.broadcasted_iota(jnp.int32, square, 1)
+    cluster_row = cluster_ref[...]
+    cluster_col = jnp.sum(
+        jnp.where(down == across, jnp.broadcast_to(cluster_row, square), 0).astype(jnp.float32),
+        axis=1, keepdims=True,
+    ).astype(jnp.int32)
+    same = cluster_col == cluster_row
+    place_row = jnp.sum(jnp.where(same & (down < across), 1.0, 0.0), axis=0, keepdims=True).astype(jnp.int32)
+    place_col = jnp.sum(jnp.where(same & (across < down), 1.0, 0.0), axis=1, keepdims=True).astype(jnp.int32)
+    slot_row = cluster_row * capacity + place_row
+
+    load.wait()
+    matrix = rows[...]
+    inverse = lax.rsqrt(jnp.sum(matrix * matrix, axis=1, keepdims=True) + 1e-06)
+    unit = (matrix * inverse).astype(jnp.bfloat16)
+
+    slot = lax.broadcasted_iota(jnp.int32, (capacity, row_count), 0)
+    lead = lax.broadcasted_iota(jnp.int32, (capacity, width), 1) == 0
+
+    def packed(step):
+        chosen = jnp.where(slot + owner_of(step) * capacity == slot_row, 1.0, 0.0)
+        block = jnp.dot(chosen.astype(jnp.bfloat16), unit, preferred_element_type=jnp.float32)
+        vacant = jnp.sum(chosen, axis=1, keepdims=True) == 0.0
+        return jnp.where(lead & vacant, 2.0, block).astype(jnp.bfloat16)
+
+    for k, step in enumerate(away):
+        outgoing[k] = packed(step)
+    own = packed((0, 0))
+    outgoing[home] = own
+
+    @pl.when(rep == 0)
+    def _():
+        gathered[me] = own
+        pl.semaphore_wait(barrier, n_shard * n_grp * n_rep - 1)
+
+    @pl.when(rep != 0)
+    def _():
+        pl.semaphore_wait(barrier, n_shard * n_grp)
+
+    def block_copy(k, step, source):
+        return pltpu.make_async_remote_copy(
+            src_ref=outgoing.at[k], dst_ref=gathered.at[source],
+            send_sem=send_sem.at[k], recv_sem=recv_sem.at[source],
+            device_id=device(step, 0),
+        )
+
+    for k, step in enumerate(away):
+        block_copy(k, step, me).start()
+
+    @pl.when(rep != 0)
+    def _():
+        block_copy(home, (0, 0), me).start()
+
+    def reply(k, core):
+        step = steps[k]
+        target = owner_of(step) * n_rep + core
+        return pltpu.make_async_remote_copy(
+            src_ref=mass.at[target // per_row], dst_ref=returned.at[my_owner],
+            send_sem=reply_send_sem.at[k * n_rep + core], recv_sem=reply_recv_sem.at[my_owner],
+            device_id=device(step, core),
+        )
+
+    pairs = [(k, core) for k in range(len(steps)) for core in range(n_rep) if (k, core) != (home, 0)]
+
+    @pl.when(rep == 0)
+    def _():
+        for k, core in reversed(pairs):
+            block_copy(k, steps[k], owner_of(steps[k]) * n_rep + core).wait_recv()
+        total = gathered.shape[0] * capacity
+        members = gathered[...].reshape(total, width)
+        live = members[:, 0:1].astype(jnp.float32) < 1.5
+        lanes = mass.shape[2]
+        group = 2 if mass.shape[0] % 2 == 0 else 1
+        for first in range(0, mass.shape[0], group):
+            span = group * lanes
+            begin = first * lanes
+            scores = lax.dot_general(
+                members, members[begin : begin + span], (((1,), (1,)), ((), ())),
+                preferred_element_type=jnp.float32,
+            )
+            query = lax.broadcasted_iota(jnp.int32, (total, span), 0)
+            key = lax.broadcasted_iota(jnp.int32, (total, span), 1) + begin
+            terms = jnp.where(live & (query != key), jnp.exp(sharpness * scores), 0.0)
+            sums = jnp.sum(terms, axis=0, keepdims=True)
+            for i in range(group):
+                mass[first + i] = sums[:, i * lanes : (i + 1) * lanes]
+        for k, core in pairs:
+            reply(k, core).start()
+        returned[my_owner] = mass[me // per_row]
+
+    def reply_from(step):
+        return pltpu.make_async_remote_copy(
+            src_ref=mass.at[0], dst_ref=returned.at[owner_of(step)],
+            send_sem=reply_send_sem.at[0], recv_sem=reply_recv_sem.at[owner_of(step)],
+            device_id=device(step, 0),
+        )
+
+    for step in reversed(away):
+        reply_from(step).wait_recv()
+
+    @pl.when(rep != 0)
+    def _():
+        reply_from((0, 0)).wait_recv()
+
+    lane = lax.broadcasted_iota(jnp.int32, (row_count, mass.shape[2]), 1)
+    picked = jnp.zeros(lane.shape, jnp.float32)
+    for owner in range(len(steps)):
+        picked = jnp.where(cluster_col == owner, returned[owner], picked)
+    mine = lane == lax.rem(me, per_row) * capacity + place_col
+    column = jnp.sum(jnp.where(mine, picked, 0.0), axis=1, keepdims=True)
+    mass_ref[...] = jnp.sum(jnp.where(down == across, column, 0.0), axis=0, keepdims=True)
+
+    for k, step in enumerate(away):
+        block_copy(k, step, me).wait_send()
+
+    @pl.when(rep != 0)
+    def _():
+        block_copy(home, (0, 0), me).wait_send()
+
+    @pl.when(rep == 0)
+    def _():
+        for k, core in pairs:
+            reply(k, core).wait_send()
+
+
+def kernel_body(sizes, embeddings, clusters):
+    n_shard, n_grp, n_rep = sizes
+    owners = n_shard * n_grp
+    sources = owners * n_rep
+    row_count, width = embeddings.shape
+    capacity = 2 * row_count // owners
+    lanes = 128
+    mass = pl.pallas_call(
+        functools.partial(kernel, sizes, capacity),
+        out_shape=jax.ShapeDtypeStruct((1, row_count), jnp.float32),
+        in_specs=[pl.BlockSpec(memory_space=pl.ANY), pl.BlockSpec(memory_space=pltpu.VMEM)],
+        out_specs=pl.BlockSpec(memory_space=pltpu.VMEM),
+        scratch_shapes=[
+            pltpu.VMEM((row_count, width), jnp.float32),
+            pltpu.VMEM((owners, capacity, width), jnp.bfloat16),
+            pltpu.VMEM((sources, capacity, width), jnp.bfloat16),
+            pltpu.VMEM((sources * capacity // lanes, 1, lanes), jnp.float32),
+            pltpu.VMEM((owners, 1, lanes), jnp.float32),
+            pltpu.SemaphoreType.DMA,
+            pltpu.SemaphoreType.DMA((owners,)),
+            pltpu.SemaphoreType.DMA((sources,)),
+            pltpu.SemaphoreType.DMA((sources,)),
+            pltpu.SemaphoreType.DMA((owners,)),
+        ],
+        compiler_params=pltpu.CompilerParams(collective_id=0, has_side_effects=True),
+    )(embeddings, clusters.reshape(1, row_count))
+    return jnp.log1p(mass.reshape(row_count))
+
+
 def solution(mesh):
+    sizes = (mesh.shape["shard"], mesh.shape["grp"], mesh.shape["rep"])
     placed = (P(("parts", "shard", "grp", "rep"), None), P(("parts", "shard", "grp", "rep"), None))
+
+    def body(embeddings, clusters):
+        row_count = embeddings.shape[0]
+        capacity = 2 * row_count // (sizes[0] * sizes[1])
+        if capacity % 16 == 0 and 128 % capacity == 0 and row_count % 128 == 0:
+            return kernel_body(sizes, embeddings, clusters)
+        return collective_body(embeddings, clusters)
+
     return jax.shard_map(
         body,
         mesh=mesh,

time: 50.5 us -> 23.3 us (0.46)
  blocking collectives: 28.7 us -> 0 us
  Pallas kernels: 0 us -> 21.9 us
  waiting for transfers between devices: 7.57 us -> 0 us
  other arithmetic: 4.43 us -> 0 us
  local copies, waits for them, and re-layouts: 4.71 us -> 1.2 us
  starting transfers between devices: 3.34 us -> 0 us
  matrix products: 1.39 us -> 0 us
    all_to_all x2 -> x0, blocking collectives: 28.7 us -> none  [the longest x1 19.1 us: body(): lax.all_to_all(outgoing.reshape(owners, capacity, feature_dim), ('shard',...]
    pallas_call x0 -> x1, Pallas kernels: none -> 21.9 us  [kernel_body(): pl.pallas_call(functools.partial(kernel, sizes, capacity), out_shape=jax....]
    all_to_all x1 -> x0, waiting for transfers between devices: 6.42 us -> none  [body(): lax.all_to_all(partial_mass.reshape(owners, capacity), ('shard', 'grp'),...]
    all_to_all x1 -> x0, starting transfers between devices: 3.33 us -> none  [body(): lax.all_to_all(partial_mass.reshape(owners, capacity), ('shard', 'grp'),...]
    all_to_all x4 -> x0, local copies, waits for them, and re-layouts: 1.79 us -> none  [the longest x2 1.2 us: body(): lax.all_to_all(partial_mass.reshape(owners, capacity), ('shard', 'grp'),...]
    dot_general x2 -> x0, matrix products: 1.39 us -> none  [the longest x1 0.88 us: body(): jnp.dot(earlier, member_table, precision=lax.Precision.HIGHEST, preferred...]
    all_to_all x2 -> x0, other arithmetic: 1.32 us -> none  [the longest x1 0.66 us: body(): lax.all_to_all(present.reshape(owners, capacity), ('shard', 'grp'), split...]
    scatter x1 -> x0, other arithmetic: 1.31 us -> none  [body(): jnp.zeros((owners * capacity, feature_dim), jnp.bfloat16).at[slot_index]]
  transfers between devices with their start and end apart: 3 -> 0, of which waited for: 2 -> 0; matrix products, arithmetic and copies ran while one was open for 4% -> 0% of each run, Pallas kernels for 0% -> 0%
where the time goes in v1:
time: 23.3 us; the launch traced here: 23.2 us
  Pallas kernels  21.9 us (94%)
  local copies, waits for them, and re-layouts  1.2 us (5%)
    pallas_call x1, Pallas kernels, kernel_body(): pl.pallas_call(functools.partial(kernel, sizes, capacity), out_shape=jax....  21.9 us
    log1p x1, local copies, waits for them, and re-layouts, kernel_body(): return jnp.log1p(mass.reshape(row_count))  1.2 us

profile of v1, /device:TPU:0, one launch (start us, length us, event | category | flops | bytes accessed | tf_op | source)
XLA Modules:
  0.0 23.2 jit_solution(11418706715096288916)
XLA Ops:
  0.0 21.9 %shard_map.28 = f32[1,128]{1,0:T(1,128)} custom-call(f32[128,768]{1,0:T(8,128)} %rows_hbm.1, s32[1,128]{1,0:T(1,128)} %bitcast.3), custom_call_target="tpu_custom_call" | custom-call | tf_op jit(solution)/shard_map/pallas_call | solution.py:274
  22.0 1.2 %log-plus-one_bitcast_fusion = f32[128]{0:T(128)} fusion(f32[1,128]{1,0:T(1,128)} %shard_map.28), kind=kLoop, calls=%fused_computation | loop fusion | bytes 1024 | tf_op jit(solution)/shard_map/log1p | solution.py:293

commit v2 on v1

--- a/solution.py
+++ b/solution.py
@@ -93,7 +93,7 @@
 
 
 def kernel(sizes, capacity, rows_hbm, cluster_ref, mass_ref, rows, outgoing, gathered, mass, returned,
-           load_sem, send_sem, recv_sem, reply_send_sem, reply_recv_sem):
+           load_sem, send_sem, recv_sem, reply_send_sem, reply_recv_sem, ahead_sem, behind_sem):
     n_shard, n_grp, n_rep = sizes
     shard, grp, rep = lax.axis_index("shard"), lax.axis_index("grp"), lax.axis_index("rep")
     row_count, width = rows.shape
@@ -124,14 +124,28 @@
     def greet(step, core):
         pl.semaphore_signal(barrier, inc=1, device_id=device(step, core))
 
-    for step in away:
-        greet(step, 0)
-
-    @pl.when(rep == 0)
-    def _():
-        for core in range(1, n_rep):
-            for step in steps:
-                greet(step, core)
+    has_next, has_last = shard + 1 < n_shard, shard > 0
+    forward, backward = (1, 0), (n_shard - 1, 0)
+
+    def greet_plane(a):
+        for b in range(n_grp):
+            if (a, b) != (0, 0):
+                greet((a, b), 0)
+
+        @pl.when(rep == 0)
+        def _():
+            for b in range(n_grp):
+                for core in range(1, n_rep):
+                    greet((a, b), core)
+
+        if a:
+            @pl.when(rep != 0)
+            def _():
+                greet((a, 0), rep)
+
+    pl.when(has_next)(lambda: greet_plane(1))
+    pl.when(has_last)(lambda: greet_plane(n_shard - 1))
+    greet_plane(0)
 
     @pl.when(rep != 0)
     def _():
@@ -168,15 +182,16 @@
         outgoing[k] = packed(step)
     own = packed((0, 0))
     outgoing[home] = own
+    beside = jnp.where(has_next, 1, 0) + jnp.where(has_last, 1, 0)
 
     @pl.when(rep == 0)
     def _():
         gathered[me] = own
-        pl.semaphore_wait(barrier, n_shard * n_grp * n_rep - 1)
-
-    @pl.when(rep != 0)
-    def _():
-        pl.semaphore_wait(barrier, n_shard * n_grp)
+        pl.semaphore_wait(barrier, beside * n_grp * n_rep + n_grp * n_rep - 1)
+
+    @pl.when(rep != 0)
+    def _():
+        pl.semaphore_wait(barrier, beside * (n_grp + 1) + n_grp)
 
     def block_copy(k, step, source):
         return pltpu.make_async_remote_copy(
@@ -185,8 +200,45 @@
             device_id=device(step, 0),
         )
 
-    for k, step in enumerate(away):
-        block_copy(k, step, me).start()
+    def send(a, b):
+        block_copy(steps.index((a, b)), (a, b), me).start()
+
+    def tell(sem, distance, step):
+        pl.semaphore_signal(sem.at[distance], inc=1, device_id=device(step, rep))
+
+    @pl.when(has_next & has_last)
+    def _():
+        if n_shard > 2:
+            tell(ahead_sem, 2, backward)
+            tell(behind_sem, 2, forward)
+
+    def send_beside(b):
+        pl.when(has_next)(lambda: send(1, b))
+        if n_shard > 2:
+            pl.when(has_last)(lambda: send(n_shard - 1, b))
+
+    send_beside(n_grp - 1)
+    for distance in range(2, n_shard):
+        @pl.when(shard + distance < n_shard)
+        def _():
+            pl.semaphore_wait(ahead_sem.at[distance], 1)
+            if distance + 1 < n_shard:
+                pl.when(has_last)(lambda: tell(ahead_sem, distance + 1, backward))
+
+        @pl.when(shard >= distance)
+        def _():
+            pl.semaphore_wait(behind_sem.at[distance], 1)
+            if distance + 1 < n_shard:
+                pl.when(has_next)(lambda: tell(behind_sem, distance + 1, forward))
+
+    for distance in reversed(range(2, n_shard)):
+        for b in reversed(range(n_grp)):
+            pl.when(shard + distance < n_shard)(lambda: send(distance, b))
+            pl.when(shard >= distance)(lambda: send(n_shard - distance, b))
+    for b in reversed(range(n_grp - 1)):
+        send_beside(b)
+    for b in range(1, n_grp):
+        send(0, b)
 
     @pl.when(rep != 0)
     def _():
@@ -287,6 +339,8 @@
             pltpu.SemaphoreType.DMA((sources,)),
             pltpu.SemaphoreType.DMA((sources,)),
             pltpu.SemaphoreType.DMA((owners,)),
+            pltpu.SemaphoreType.REGULAR((n_shard,)),
+            pltpu.SemaphoreType.REGULAR((n_shard,)),
         ],
         compiler_params=pltpu.CompilerParams(collective_id=0, has_side_effects=True),
     )(embeddings, clusters.reshape(1, row_count))

time: 23.3 us -> 22.8 us (0.979)
  Pallas kernels: 21.9 us -> 21.4 us
    pallas_call x1, Pallas kernels: 21.9 us -> 21.4 us  [kernel_body(): pl.pallas_call(functools.partial(kernel, sizes, capacity), out_shape=jax....]
where the time goes in v2:
time: 22.8 us; the launch traced here: 22.6 us
  Pallas kernels  21.4 us (94%)
  local copies, waits for them, and re-layouts  1.2 us (5%)
    pallas_call x1, Pallas kernels, kernel_body(): pl.pallas_call(functools.partial(kernel, sizes, capacity), out_shape=jax....  21.4 us
    log1p x1, local copies, waits for them, and re-layouts, kernel_body(): return jnp.log1p(mass.reshape(row_count))  1.2 us

profile of v2, /device:TPU:0, one launch (start us, length us, event | category | flops | bytes accessed | tf_op | source)
XLA Modules:
  0.0 22.6 jit_solution(2743189815894053528)
XLA Ops:
  0.0 21.4 %shard_map.28 = f32[1,128]{1,0:T(1,128)} custom-call(f32[128,768]{1,0:T(8,128)} %rows_hbm.1, s32[1,128]{1,0:T(1,128)} %bitcast.3), custom_call_target="tpu_custom_call" | custom-call | tf_op jit(solution)/shard_map/pallas_call | solution.py:326
  21.4 1.2 %log-plus-one_bitcast_fusion = f32[128]{0:T(128)} fusion(f32[1,128]{1,0:T(1,128)} %shard_map.28), kind=kLoop, calls=%fused_computation | loop fusion | bytes 1024 | tf_op jit(solution)/shard_map/log1p | solution.py:347

commit v3 on v2

--- a/solution.py
+++ b/solution.py
@@ -257,26 +257,41 @@
 
     @pl.when(rep == 0)
     def _():
-        for k, core in reversed(pairs):
-            block_copy(k, steps[k], owner_of(steps[k]) * n_rep + core).wait_recv()
-        total = gathered.shape[0] * capacity
-        members = gathered[...].reshape(total, width)
-        live = members[:, 0:1].astype(jnp.float32) < 1.5
+        half = gathered.shape[0] // 2
+        near = jnp.where(2 * shard >= n_shard, half, 0)
+        far = half - near
+        span = half * capacity
+
+        def arrivals(wanted):
+            for k, core in reversed(pairs):
+                source = owner_of(steps[k]) * n_rep + core
+                here = (source >= near) & (source < near + half)
+                pl.when(here if wanted else jnp.logical_not(here))(block_copy(k, steps[k], source).wait_recv)
+
+        def sums(queries, keys, same_half):
+            scores = lax.dot_general(
+                queries, keys, (((1,), (1,)), ((), ())), preferred_element_type=jnp.float32
+            )
+            counted = queries[:, 0:1].astype(jnp.float32) < 1.5
+            if same_half:
+                counted = counted & (
+                    lax.broadcasted_iota(jnp.int32, scores.shape, 0)
+                    != lax.broadcasted_iota(jnp.int32, scores.shape, 1)
+                )
+            return jnp.sum(jnp.where(counted, jnp.exp(sharpness * scores), 0.0), axis=0, keepdims=True)
+
+        arrivals(True)
+        mine = gathered[pl.ds(near, half)].reshape(span, width)
+        partial = sums(mine, mine, True)
+        arrivals(False)
+        theirs = gathered[pl.ds(far, half)].reshape(span, width)
         lanes = mass.shape[2]
-        group = 2 if mass.shape[0] % 2 == 0 else 1
-        for first in range(0, mass.shape[0], group):
-            span = group * lanes
-            begin = first * lanes
-            scores = lax.dot_general(
-                members, members[begin : begin + span], (((1,), (1,)), ((), ())),
-                preferred_element_type=jnp.float32,
-            )
-            query = lax.broadcasted_iota(jnp.int32, (total, span), 0)
-            key = lax.broadcasted_iota(jnp.int32, (total, span), 1) + begin
-            terms = jnp.where(live & (query != key), jnp.exp(sharpness * scores), 0.0)
-            sums = jnp.sum(terms, axis=0, keepdims=True)
-            for i in range(group):
-                mass[first + i] = sums[:, i * lanes : (i + 1) * lanes]
+        for first, total in (
+            (near, partial + sums(theirs, mine, False)),
+            (far, sums(mine, theirs, False) + sums(theirs, theirs, True)),
+        ):
+            for i in range(span // lanes):
+                mass[first // per_row + i] = total[:, i * lanes : (i + 1) * lanes]
         for k, core in pairs:
             reply(k, core).start()
         returned[my_owner] = mass[me // per_row]
@@ -353,8 +368,9 @@
 
     def body(embeddings, clusters):
         row_count = embeddings.shape[0]
-        capacity = 2 * row_count // (sizes[0] * sizes[1])
-        if capacity % 16 == 0 and 128 % capacity == 0 and row_count % 128 == 0:
+        owners = sizes[0] * sizes[1]
+        capacity = 2 * row_count // owners
+        if capacity % 16 == 0 and 128 % capacity == 0 and row_count % 128 == 0 and owners * capacity % 128 == 0:
             return kernel_body(sizes, embeddings, clusters)
         return collective_body(embeddings, clusters)
 

time: 22.8 us -> 22.7 us (level)
  no operation moved by 1% of the time
where the time goes in v3:
time: 22.7 us; the launch traced here: 22.5 us
  Pallas kernels  21.3 us (94%)
  local copies, waits for them, and re-layouts  1.2 us (5%)
    pallas_call x1, Pallas kernels, kernel_body(): pl.pallas_call(functools.partial(kernel, sizes, capacity), out_shape=jax....  21.3 us
    log1p x1, local copies, waits for them, and re-layouts, kernel_body(): return jnp.log1p(mass.reshape(row_count))  1.2 us

profile of v3, /device:TPU:0, one launch (start us, length us, event | category | flops | bytes accessed | tf_op | source)
XLA Modules:
  0.0 22.5 jit_solution(1640028450499203075)
XLA Ops:
  0.0 21.3 %shard_map.28 = f32[1,128]{1,0:T(1,128)} custom-call(f32[128,768]{1,0:T(8,128)} %rows_hbm.1, s32[1,128]{1,0:T(1,128)} %bitcast.3), custom_call_target="tpu_custom_call" | custom-call | tf_op jit(solution)/shard_map/pallas_call | solution.py:341
  21.3 1.2 %log-plus-one_bitcast_fusion = f32[128]{0:T(128)} fusion(f32[1,128]{1,0:T(1,128)} %shard_map.28), kind=kLoop, calls=%fused_computation | loop fusion | bytes 1024 | tf_op jit(solution)/shard_map/log1p | solution.py:362
